TPU v7x, 256 devices: a whole 4x4x8 slice. The times are simulated.
256 devices in a mesh: section: 2 (over y_hi), seq: 32 (over x, z), chan: 4 (over y_lo, core).
Axes of the slice: x: 4, y: 4 (y_hi: 2, y_lo: 2; y = y_hi * 2 + y_lo), z: 8, core: 2. Of those that a mesh axis runs over, the one named last changes fastest.
Arguments:
- bases: int32 [2, 2097152], P('section', 'seq'), may hold values from 0 to 3
- stem_embedding_weight: bfloat16 [512, 1536], P(None, 'chan'), may hold values from -1.64443437 to 1.64443437
- gains: float32 [3, 1536], replicated, may hold values from 0.1 to 1.9
- conv_weight: bfloat16 [3, 3, 1536, 1536], P(None, None, None, 'chan'), may hold values from -0.09375 to 0.09375
- dec_weight: bfloat16 [1536, 384], P('chan'), may hold values from -0.3125 to 0.3125
- upstream: bfloat16 [2, 16384, 1536], P('section', 'seq', 'chan'), may hold values from -0.032958984 to 0.032958984
Outputs:
- decoded: bfloat16 [2, 16384, 1536], P('section', 'seq', 'chan')
- weight_grad: float32 [1536, 384], P('chan')
All inputs are finite; a program needn't handle non-finite values.
Results may differ from a plain program's by a relative error of at most 0.0076.
Values may be sent and summed in bfloat16 or wider, within the bound.
No kernel may reach another device: no remote copies, remote signals or barrier semaphores. Data moves between devices by JAX's collectives and lax.ppermute only.
A program may use at most 128 MiB of HBM per device.

v0:
```python
import jax
import jax.numpy as jnp
from jax import lax
from jax.sharding import PartitionSpec as P

PATCH = 128
FIRST_DILATION0 = 2
EPSILON = 1e-06


def with_halo(shard, sides, width):
    for axis, dim in sides:
        size, length = (lax.axis_size(axis), shard.shape[dim])
        up = [(i, (i + 1) % size) for i in range(size - 1)]
        down = [(j, i) for i, j in up]
        last = lax.slice_in_dim(shard, length - width, length, axis=dim)
        initial = lax.slice_in_dim(shard, 0, width, axis=dim)
        before = lax.ppermute(last, axis, up)
        after = lax.ppermute(initial, axis, down)
        shard = jnp.concatenate([before, shard, after], axis=dim)
    return shard


def activate(rows, gain_row):
    widened = rows.astype(jnp.float32)
    inverse_rms = lax.rsqrt(jnp.mean(widened * widened, axis=-1, keepdims=True) + EPSILON)
    return jax.nn.gelu(widened * inverse_rms * gain_row).astype(jnp.bfloat16)


def apply_convolution(padded, kernel_taps, dilation_step, row_count):
    update = jnp.dot(padded[0:row_count], kernel_taps[0], preferred_element_type=jnp.float32)
    for offset in range(1, kernel_taps.shape[0]):
        start = offset * dilation_step
        update = update + jnp.dot(
            padded[start : start + row_count],
            kernel_taps[offset],
            preferred_element_type=jnp.float32,
        )
    return update


def body(bases, stem_embedding_weight, gains, conv_weight, dec_weight, upstream):
    row_count = upstream.shape[1]
    letters = bases.reshape(row_count, PATCH)
    onehot = letters[:, :, None] == jnp.arange(4, dtype=jnp.int32)[None, None, :]
    onehot = onehot.astype(jnp.bfloat16).reshape(row_count, PATCH * 4)
    stream = jnp.dot(onehot, stem_embedding_weight, preferred_element_type=jnp.float32).astype(
        jnp.bfloat16
    )
    for tower_layer_index in range(conv_weight.shape[0]):
        dilation_step = FIRST_DILATION0 * 2**tower_layer_index
        full_rows = lax.all_gather(stream, "chan", axis=1, tiled=True)
        padded = with_halo(
            activate(full_rows, gains[tower_layer_index]), (("seq", 0),), dilation_step
        )
        update = apply_convolution(padded, conv_weight[tower_layer_index], dilation_step, row_count)
        stream = (stream.astype(jnp.float32) + update).astype(jnp.bfloat16)
    decoded = jnp.dot(stream, dec_weight, preferred_element_type=jnp.float32).astype(jnp.bfloat16)
    upstream_rows = upstream[0]
    contract_row_pairs = (((0,), (0,)), ((), ()))
    partial_grad = lax.dot_general(
        stream, upstream_rows, contract_row_pairs, preferred_element_type=jnp.float32
    )
    weight_grad = lax.psum(partial_grad, ("section", "seq"))
    return (decoded[None], weight_grad)


def solution(mesh):
    placed = (
        P("section", "seq"),
        P(None, "chan"),
        P(),
        P(None, None, None, "chan"),
        P("chan", None),
        P("section", "seq", "chan"),
    )
    return jax.shard_map(
        body,
        mesh=mesh,
        in_specs=placed,
        out_specs=(P("section", "seq", "chan"), P("chan", None)),
        check_vma=False,
    )
```

profile of v0, /device:TPU:24, one launch (start us, length us, event | category | flops | bytes accessed | tf_op | source)
XLA Modules:
  0.0 813.8 jit_solution(4729358638135030658)
XLA Ops:
  7.4 1.1 copy.8
  8.6 0.4 eq.24
  9.0 1.3 convolution_convert_fusion.1
  10.5 29.4 %all-gather.4.cloned.1.call-done = bf16[512,1536]{1,0:T(8,128)(2,1)} async-done(((bf16[512,384]{1,0:T(8,128)(2,1)}), bf16[512,1536]{1,0:T(8,128)(2,1)}) %all-gather.4.cloned.1.call-update) | async-done | bytes 1572880 | tf_op jit(solution)/shard_map/all_gather | solution.py:52
  39.8 1.8 fusion
  41.6 2.8 fusion.4
  44.5 3.5 collective-permute-start
  47.9 1.3 collective-permute-start.1
  49.2 2.2 fusion.60
  51.5 2.0 collective-permute-done.1
  53.4 2.3 fusion.38
  55.7 3.1 fusion.49
  58.8 28.8 %all-gather.6.cloned.1.call-done = bf16[512,1536]{1,0:T(8,128)(2,1)} async-done(((bf16[512,384]{1,0:T(8,128)(2,1)}), bf16[512,1536]{1,0:T(8,128)(2,1)}) %all-gather.6.cloned.1.call-update) | async-done | bytes 1572880 | tf_op jit(solution)/shard_map/all_gather | solution.py:52
  87.6 1.8 fusion.9
  89.4 2.8 fusion.13
  92.2 1.3 collective-permute-start.3
  93.5 2.2 fusion.56
  95.8 4.7 collective-permute-start.2
  100.5 2.3 fusion.34
  102.8 3.0 add_convert_fusion.1
  105.9 29.4 %all-gather.8.cloned.1.call-done = bf16[512,1536]{1,0:T(8,128)(2,1)} async-done(((bf16[512,384]{1,0:T(8,128)(2,1)}), bf16[512,1536]{1,0:T(8,128)(2,1)}) %all-gather.8.cloned.1.call-update) | async-done | bytes 1572880 | tf_op jit(solution)/shard_map/all_gather | solution.py:52
  135.3 1.8 fusion.18
  137.1 2.8 fusion.22
  139.9 1.5 collective-permute-start.5
  141.4 2.2 fusion.52
  143.7 4.7 collective-permute-start.4
  148.4 2.2 fusion.30
  150.7 2.3 add_convert_fusion
  153.0 1.2 fusion.74
  154.3 1.1 fusion.50
  155.4 649.9 %all-reduce.2.cloned.1.call-done = f32[384,384]{1,0:T(8,128)} async-done(((f32[384,384]{1,0:T(8,128)}), f32[384,384]{1,0:T(8,128)}) %all-reduce.2.cloned.1.call-update) | async-done | bytes 589840 | tf_op jit(solution)/shard_map/psum | solution.py:64
  805.3 1.9 copy.10
  (37 shorter events, 0.7 us)
Async XLA Ops:
  7.2 1.8 copy-start
  7.2 3.2 copy-start.6
  7.2 32.7 %all-gather.4.cloned.1.call-start = ((), (), s32[]{:S(2)}) async-start(), calls=%async_computation | async-start | bytes 1966080 | tf_op jit(solution)/shard_map/all_gather | solution.py:52
  10.4 77.3 %all-gather.6.cloned.1.call-start = ((), (), s32[]{:S(2)}) async-start(), calls=%async_computation.1 | async-start | bytes 1966080 | tf_op jit(solution)/shard_map/all_gather | solution.py:52
  44.5 11.2 %collective-permute-start = (bf16[2,1536]{1,0:T(2,128)(2,1)S(1)}, bf16[2,1536]{1,0:T(2,128)(2,1)S(1)}, u32[]{:S(2)}, u32[]{:S(2)}) collective-permute-start(bf16[2,1536]{1,0:T(2,128)(2,1)S(1)} %get-tuple-element.9), channel_id=1, source_target_pairs={{0,4},{4,8},{8,12},{12,16},{16,20},{20,24},{24,28},{28,32},{32,36}... | collective-permute-start | bytes 18440 | tf_op jit(solution)/shard_map/ppermute | solution.py:18
  47.9 5.5 collective-permute-start.1
  51.5 4.2 copy-start.1
  58.8 76.5 %all-gather.8.cloned.1.call-start = ((), (), s32[]{:S(2)}) async-start(), calls=%async_computation.2 | async-start | bytes 1966080 | tf_op jit(solution)/shard_map/all_gather | solution.py:52
  92.2 8.3 %collective-permute-start.3 = (bf16[4,1536]{1,0:T(4,128)(2,1)S(1)}, bf16[4,1536]{1,0:T(4,128)(2,1)S(1)}, u32[]{:S(2)}, u32[]{:S(2)}) collective-permute-start(bf16[4,1536]{1,0:T(4,128)(2,1)S(1)} %get-tuple-element.8), channel_id=1, source_target_pairs={{4,0},{8,4},{12,8},{16,12},{20,16},{24,20},{28,24},{32,28},{36,32}... | collective-permute-start | bytes 36872 | tf_op jit(solution)/shard_map/ppermute | solution.py:19
  95.8 7.0 copy-start.3
  95.8 7.0 collective-permute-start.2
  105.9 699.5 %all-reduce.2.cloned.1.call-start = ((), (), s32[]{:S(2)}) async-start(), calls=%async_computation.3 | async-start | bytes 1179648 | tf_op jit(solution)/shard_map/psum | solution.py:64
  139.9 8.4 %collective-permute-start.5 = (bf16[8,1536]{1,0:T(8,128)(2,1)S(1)}, bf16[8,1536]{1,0:T(8,128)(2,1)S(1)}, u32[]{:S(2)}, u32[]{:S(2)}) collective-permute-start(bf16[8,1536]{1,0:T(8,128)(2,1)S(1)} %get-tuple-element.6), channel_id=1, source_target_pairs={{4,0},{8,4},{12,8},{16,12},{20,16},{24,20},{28,24},{32,28},{36,32}... | collective-permute-start | bytes 73736 | tf_op jit(solution)/shard_map/ppermute | solution.py:19
  143.7 7.0 copy-start.2
  143.7 7.0 collective-permute-start.4
  150.6 2.4 copy-start.4
  150.6 3.6 copy-start.5
Sparse Core Ops, SparseCore 0:
  10.5 29.3 all-gather.3
  58.9 28.6 all-gather.5
  106.0 29.3 all-gather.7
  154.4 650.8 all-reduce.1
where the time goes:
time: 815 us; the launch traced here: 814 us
  waiting for transfers between devices  740 us (91%)
  matrix products  25.6 us (3%)
  starting transfers between devices  17 us (2%)
  between operations  14.1 us (2%)
  other arithmetic  13.7 us (2%)
    psum x1, waiting for transfers between devices, body(): weight_grad = lax.psum(partial_grad, ('section', 'seq'))  650 us
    all_gather x3, waiting for transfers between devices, body(): full_rows = lax.all_gather(stream, 'chan', axis=1, tiled=True)  87.6 us
  transfers between devices with their start and end apart: 10, of which 5 were waited for; matrix products, arithmetic and copies ran while one was open for 2% of the time, Pallas kernels for 0%

commit v1 on v0

--- a/solution.py
+++ b/solution.py
@@ -61,7 +61,7 @@
     partial_grad = lax.dot_general(
         stream, upstream_rows, contract_row_pairs, preferred_element_type=jnp.float32
     )
-    weight_grad = lax.psum(partial_grad, ("section", "seq"))
+    weight_grad = lax.psum(lax.psum(partial_grad, "section"), "seq")
     return (decoded[None], weight_grad)
 
 

time: 815 us -> 360 us (0.44)
  waiting for transfers between devices: 740 us -> 285 us
    psum x1 -> x2, waiting for transfers between devices: 650 us -> 196 us  [body(): weight_grad = lax.psum(lax.psum(partial_grad, 'section'), 'seq')]
  transfers between devices with their start and end apart: 10 -> 11, of which waited for: 5 -> 6; matrix products, arithmetic and copies ran while one was open for 2% -> 4% of each run, Pallas kernels for 0% -> 0%
where the time goes in v1:
time: 360 us; the launch traced here: 359 us
  waiting for transfers between devices  285 us (79%)
  matrix products  25.6 us (7%)
  starting transfers between devices  17.1 us (5%)
  between operations  14.1 us (4%)
  other arithmetic  13.7 us (4%)
  local copies, waits for them, and re-layouts  3.78 us (1%)
    psum x2, waiting for transfers between devices, body(): weight_grad = lax.psum(lax.psum(partial_grad, 'section'), 'seq')  196 us
    all_gather x3, waiting for transfers between devices, body(): full_rows = lax.all_gather(stream, 'chan', axis=1, tiled=True)  87.6 us
    dot_general x6, matrix products, apply_convolution(): jnp.dot(padded[start:start + row_count], kernel_taps[offset], preferred_e...  13.5 us
    ppermute x3, starting transfers between devices, with_halo(): before = lax.ppermute(last, axis, up)  12.8 us
    dot_general x3, matrix products, apply_convolution(): jnp.dot(padded[0:row_count], kernel_taps[0], preferred_element_type=jnp.f...  8.45 us
    convert_element_type x3, other arithmetic, activate(): return jax.nn.gelu(widened * inverse_rms * gain_row).astype(jnp.bfloat16)  8.35 us
  transfers between devices with their start and end apart: 11, of which 6 were waited for; matrix products, arithmetic and copies ran while one was open for 4% of the time, Pallas kernels for 0%

profile of v1, /device:TPU:24, one launch (start us, length us, event | category | flops | bytes accessed | tf_op | source)
XLA Modules:
  0.0 359.5 jit_solution(875136142565981440)
XLA Ops:
  7.4 1.1 copy.8
  9.0 1.3 convolution_convert_fusion.1
  10.5 29.4 %all-gather.4.cloned.1.call-done = bf16[512,1536]{1,0:T(8,128)(2,1)} async-done(((bf16[512,384]{1,0:T(8,128)(2,1)}), bf16[512,1536]{1,0:T(8,128)(2,1)}) %all-gather.4.cloned.1.call-update) | async-done | bytes 1572880 | tf_op jit(solution)/shard_map/all_gather | solution.py:52
  39.8 1.8 fusion
  41.6 2.8 fusion.4
  44.5 3.5 collective-permute-start
  47.9 1.3 collective-permute-start.1
  49.2 2.2 fusion.60
  51.5 2.0 collective-permute-done.1
  53.4 2.3 fusion.38
  55.7 3.1 fusion.49
  58.8 28.8 %all-gather.6.cloned.1.call-done = bf16[512,1536]{1,0:T(8,128)(2,1)} async-done(((bf16[512,384]{1,0:T(8,128)(2,1)}), bf16[512,1536]{1,0:T(8,128)(2,1)}) %all-gather.6.cloned.1.call-update) | async-done | bytes 1572880 | tf_op jit(solution)/shard_map/all_gather | solution.py:52
  87.6 1.8 fusion.9
  89.4 2.8 fusion.13
  92.2 1.3 collective-permute-start.3
  93.5 2.2 fusion.56
  95.8 4.7 %collective-permute-start.2 = (bf16[4,1536]{1,0:T(4,128)(2,1)S(1)}, bf16[4,1536]{1,0:T(4,128)(2,1)S(1)}, u32[]{:S(2)}, u32[]{:S(2)}) collective-permute-start(bf16[4,1536]{1,0:T(4,128)(2,1)S(1)} %get-tuple-element.7), channel_id=1, source_target_pairs={{0,4},{4,8},{8,12},{12,16},{16,20},{20,24},{24,28},{28,32},{32,36}... | collective-permute-start | bytes 36872 | tf_op jit(solution)/shard_map/ppermute | solution.py:18
  100.5 2.3 fusion.34
  102.8 3.0 add_convert_fusion.1
  105.9 29.4 %all-gather.8.cloned.1.call-done = bf16[512,1536]{1,0:T(8,128)(2,1)} async-done(((bf16[512,384]{1,0:T(8,128)(2,1)}), bf16[512,1536]{1,0:T(8,128)(2,1)}) %all-gather.8.cloned.1.call-update) | async-done | bytes 1572880 | tf_op jit(solution)/shard_map/all_gather | solution.py:52
  135.3 1.8 fusion.18
  137.1 2.8 fusion.22
  139.9 1.5 collective-permute-start.5
  141.4 2.2 fusion.52
  143.7 4.7 %collective-permute-start.4 = (bf16[8,1536]{1,0:T(8,128)(2,1)S(1)}, bf16[8,1536]{1,0:T(8,128)(2,1)S(1)}, u32[]{:S(2)}, u32[]{:S(2)}) collective-permute-start(bf16[8,1536]{1,0:T(8,128)(2,1)S(1)} %get-tuple-element.5), channel_id=1, source_target_pairs={{0,4},{4,8},{8,12},{12,16},{16,20},{20,24},{24,28},{28,32},{32,36}... | collective-permute-start | bytes 73736 | tf_op jit(solution)/shard_map/ppermute | solution.py:18
  148.4 2.2 fusion.30
  150.7 2.3 add_convert_fusion
  153.0 1.2 fusion.74
  154.3 44.5 %all-reduce.3.cloned.1.call-done = f32[384,384]{1,0:T(8,128)} async-done(((f32[384,384]{1,0:T(8,128)}), f32[384,384]{1,0:T(8,128)}) %all-reduce.3.cloned.1.call-update) | async-done | bytes 589840 | tf_op jit(solution)/shard_map/psum | solution.py:64
  198.9 1.1 fusion.50
  200.0 151.0 %all-reduce.5.cloned.1.call-done = f32[384,384]{1,0:T(8,128)} async-done(((f32[384,384]{1,0:T(8,128)}), f32[384,384]{1,0:T(8,128)}) %all-reduce.5.cloned.1.call-update) | async-done | bytes 589840 | tf_op jit(solution)/shard_map/psum | solution.py:64
  351.0 1.9 copy.11
  (40 shorter events, 1.1 us)
Async XLA Ops:
  7.2 1.8 copy-start
  7.2 3.2 copy-start.6
  7.2 32.7 %all-gather.4.cloned.1.call-start = ((), (), s32[]{:S(2)}) async-start(), calls=%async_computation | async-start | bytes 1966080 | tf_op jit(solution)/shard_map/all_gather | solution.py:52
  10.4 77.3 %all-gather.6.cloned.1.call-start = ((), (), s32[]{:S(2)}) async-start(), calls=%async_computation.1 | async-start | bytes 1966080 | tf_op jit(solution)/shard_map/all_gather | solution.py:52
  44.5 11.2 %collective-permute-start = (bf16[2,1536]{1,0:T(2,128)(2,1)S(1)}, bf16[2,1536]{1,0:T(2,128)(2,1)S(1)}, u32[]{:S(2)}, u32[]{:S(2)}) collective-permute-start(bf16[2,1536]{1,0:T(2,128)(2,1)S(1)} %get-tuple-element.9), channel_id=1, source_target_pairs={{0,4},{4,8},{8,12},{12,16},{16,20},{20,24},{24,28},{28,32},{32,36}... | collective-permute-start | bytes 18440 | tf_op jit(solution)/shard_map/ppermute | solution.py:18
  47.9 5.5 %collective-permute-start.1 = (bf16[2,1536]{1,0:T(2,128)(2,1)S(1)}, bf16[2,1536]{1,0:T(2,128)(2,1)S(1)}, u32[]{:S(2)}, u32[]{:S(2)}) collective-permute-start(bf16[2,1536]{1,0:T(2,128)(2,1)S(1)} %get-tuple-element.10), channel_id=1, source_target_pairs={{4,0},{8,4},{12,8},{16,12},{20,16},{24,20},{28,24},{32,28},{36,32}... | collective-permute-start | bytes 18440 | tf_op jit(solution)/shard_map/ppermute | solution.py:19
  51.5 4.2 %copy-start.1 = (bf16[512,384]{1,0:T(8,128)(2,1)S(1)}, bf16[512,384]{1,0:T(8,128)(2,1)}, u32[]{:S(2)}) copy-start(bf16[512,384]{1,0:T(8,128)(2,1)} %convolution_convert_fusion.1) | copy-start | bytes 1179652
  58.8 76.5 %all-gather.8.cloned.1.call-start = ((), (), s32[]{:S(2)}) async-start(), calls=%async_computation.2 | async-start | bytes 1966080 | tf_op jit(solution)/shard_map/all_gather | solution.py:52
  92.2 8.3 %collective-permute-start.3 = (bf16[4,1536]{1,0:T(4,128)(2,1)S(1)}, bf16[4,1536]{1,0:T(4,128)(2,1)S(1)}, u32[]{:S(2)}, u32[]{:S(2)}) collective-permute-start(bf16[4,1536]{1,0:T(4,128)(2,1)S(1)} %get-tuple-element.8), channel_id=1, source_target_pairs={{4,0},{8,4},{12,8},{16,12},{20,16},{24,20},{28,24},{32,28},{36,32}... | collective-permute-start | bytes 36872 | tf_op jit(solution)/shard_map/ppermute | solution.py:19
  95.8 7.0 %copy-start.3 = (bf16[512,384]{1,0:T(8,128)(2,1)S(1)}, bf16[512,384]{1,0:T(8,128)(2,1)}, u32[]{:S(2)}) copy-start(bf16[512,384]{1,0:T(8,128)(2,1)} %fusion.49) | copy-start | bytes 1179652
  95.8 7.0 %collective-permute-start.2 = (bf16[4,1536]{1,0:T(4,128)(2,1)S(1)}, bf16[4,1536]{1,0:T(4,128)(2,1)S(1)}, u32[]{:S(2)}, u32[]{:S(2)}) collective-permute-start(bf16[4,1536]{1,0:T(4,128)(2,1)S(1)} %get-tuple-element.7), channel_id=1, source_target_pairs={{0,4},{4,8},{8,12},{12,16},{16,20},{20,24},{24,28},{28,32},{32,36}... | collective-permute-start | bytes 36872 | tf_op jit(solution)/shard_map/ppermute | solution.py:18
  105.9 93.0 %all-reduce.3.cloned.1.call-start = ((), (), s32[]{:S(2)}) async-start(), calls=%async_computation.3 | async-start | bytes 1179648 | tf_op jit(solution)/shard_map/psum | solution.py:64
  139.9 8.4 %collective-permute-start.5 = (bf16[8,1536]{1,0:T(8,128)(2,1)S(1)}, bf16[8,1536]{1,0:T(8,128)(2,1)S(1)}, u32[]{:S(2)}, u32[]{:S(2)}) collective-permute-start(bf16[8,1536]{1,0:T(8,128)(2,1)S(1)} %get-tuple-element.6), channel_id=1, source_target_pairs={{4,0},{8,4},{12,8},{16,12},{20,16},{24,20},{28,24},{32,28},{36,32}... | collective-permute-start | bytes 73736 | tf_op jit(solution)/shard_map/ppermute | solution.py:19
  143.7 7.0 %copy-start.2 = (bf16[512,384]{1,0:T(8,128)(2,1)S(1)}, bf16[512,384]{1,0:T(8,128)(2,1)}, u32[]{:S(2)}) copy-start(bf16[512,384]{1,0:T(8,128)(2,1)} %add_convert_fusion.1) | copy-start | bytes 1179652
  143.7 7.0 %collective-permute-start.4 = (bf16[8,1536]{1,0:T(8,128)(2,1)S(1)}, bf16[8,1536]{1,0:T(8,128)(2,1)S(1)}, u32[]{:S(2)}, u32[]{:S(2)}) collective-permute-start(bf16[8,1536]{1,0:T(8,128)(2,1)S(1)} %get-tuple-element.5), channel_id=1, source_target_pairs={{0,4},{4,8},{8,12},{12,16},{16,20},{20,24},{24,28},{28,32},{32,36}... | collective-permute-start | bytes 73736 | tf_op jit(solution)/shard_map/ppermute | solution.py:18
  150.6 2.4 copy-start.4
  150.6 48.2 %copy-start.5 = (bf16[384,384]{1,0:T(8,128)(2,1)S(1)}, bf16[384,384]{1,0:T(8,128)(2,1)}, u32[]{:S(2)}) copy-start(bf16[384,384]{1,0:T(8,128)(2,1)} %param.10) | copy-start | bytes 884740
  154.3 196.7 %all-reduce.5.cloned.1.call-start = ((), (), s32[]{:S(2)}) async-start(), calls=%async_computation.4 | async-start | bytes 1179648 | tf_op jit(solution)/shard_map/psum | solution.py:64
Sparse Core Ops, SparseCore 0:
  10.5 29.3 all-gather.3
  58.9 28.6 all-gather.5
  106.0 29.3 all-gather.7
  154.4 44.3 all-reduce.2
  202.4 148.5 all-reduce.4
